TPU v7x, 32 devices: a whole 2x2x4 slice. The times are simulated.
32 devices in a mesh: dp: 8 (over z, y), mp: 4 (over x, core).
Axes of the slice: x: 2, y: 2, z: 4, core: 2. Of those that a mesh axis runs over, the one named last changes fastest.
Arguments:
- output_gradient: bfloat16 [1536, 3584], P('dp', 'mp'), may hold values from -6 to 6
- gate_preactivation: bfloat16 [1536, 9984], P('dp', 'mp'), may hold values from -8 to 8
- up_preactivation: bfloat16 [1536, 9984], P('dp', 'mp'), may hold values from -6 to 6
- down_weight: bfloat16 [9984, 3584], P('mp'), may hold values from -0.0625 to 0.0625
- adapter_first: bfloat16 [9984, 96], P('mp'), may hold values from -0.0625 to 0.0625
- adapter_second: bfloat16 [96, 3584], replicated, may hold values from -0.09375 to 0.09375
- plan: int32 [192], P('dp'), may hold values from 0 to 7, as said below
Outputs:
- grad_gate: bfloat16 [1536, 9984], P('dp', 'mp')
- grad_up: bfloat16 [1536, 9984], P('dp', 'mp')
- grad_a: float32 [4, 2496, 96], P('mp', 'dp')
- grad_b: float32 [96, 3584], P('dp')
Inputs may be any that keep to these rules, and one draw needn't show every extreme that they name: Every owner 0 to 7 is named by exactly 24 blocks; of the 24 blocks of one device (plan rows of one index of dp) at most 3 name the same owner, and in every draw some device's blocks name one owner exactly 3 times.
All inputs are finite; a program needn't handle non-finite values.
Results may differ from a plain program's by a relative error of at most 0.005.
Values may be sent and summed in bfloat16 or wider, within the bound.
No kernel may reach another device: no remote copies, remote signals or barrier semaphores. Data moves between devices by JAX's collectives and lax.ppermute only.
A program may use at most 64 MiB of HBM per device.

v0:
```python
import jax
import jax.numpy as jnp
from jax import lax
from jax.sharding import PartitionSpec as P


def body(
    output_gradient,
    gate_preactivation,
    up_preactivation,
    down_weight,
    adapter_first,
    adapter_second,
    plan,
):
    groups = lax.axis_size("dp")
    owned = plan.shape[0]
    capacity = -(-owned // groups)
    tokens_here = output_gradient.shape[0]
    feature_cols = output_gradient.shape[1]
    block_width = tokens_here // owned * feature_cols
    slot_count = groups * capacity
    positions = jnp.arange(owned, dtype=jnp.int32)
    earlier = (plan[None, :] == plan[:, None]) & (positions[None, :] < positions[:, None])
    target = plan * capacity + jnp.sum(earlier.astype(jnp.int32), axis=1)
    sending = target[None, :] == jnp.arange(slot_count, dtype=jnp.int32)[:, None]
    outgoing = jnp.dot(
        sending.astype(jnp.bfloat16),
        output_gradient.reshape(owned, block_width),
        preferred_element_type=jnp.float32,
    ).astype(jnp.bfloat16)
    filled = jnp.sum(sending.astype(jnp.float32), axis=1).astype(jnp.bfloat16)
    arrived, present = (
        lax.all_to_all(outgoing, "dp", split_axis=0, concat_axis=0, tiled=True),
        lax.all_to_all(filled, "dp", split_axis=0, concat_axis=0, tiled=True),
    )
    present_flag = present.astype(jnp.int32)
    ranking = jnp.cumsum(present_flag) - 1
    keeping = (ranking[None, :] == positions[:, None]) & (present_flag[None, :] > 0)
    packed_tokens = (
        jnp.dot(keeping.astype(jnp.bfloat16), arrived, preferred_element_type=jnp.float32)
        .astype(jnp.bfloat16)
        .reshape(tokens_here, feature_cols)
    )
    feature_rows = lax.all_gather(packed_tokens, "mp", axis=1, tiled=True)
    gate_vals = gate_preactivation.astype(jnp.float32)
    up_vals = up_preactivation.astype(jnp.float32)
    sigmoid_gate = jax.nn.sigmoid(gate_vals)
    silu_gate = gate_vals * sigmoid_gate
    hidden_units = (silu_gate * up_vals).astype(jnp.bfloat16)
    low_rank_piece = jnp.dot(hidden_units, adapter_first, preferred_element_type=jnp.float32)
    low_rank_rows = lax.psum(low_rank_piece, "mp").astype(jnp.bfloat16)
    passed_through = lax.dot_general(
        feature_rows, adapter_second, (((1,), (1,)), ((), ())), preferred_element_type=jnp.float32
    ).astype(jnp.bfloat16)
    grad_a_rows = lax.psum_scatter(
        lax.dot_general(
            hidden_units,
            passed_through,
            (((0,), (0,)), ((), ())),
            preferred_element_type=jnp.float32,
        ),
        "dp",
        scatter_dimension=0,
        tiled=True,
    )
    part_rows = lax.psum_scatter(
        lax.dot_general(
            low_rank_rows,
            packed_tokens,
            (((0,), (0,)), ((), ())),
            preferred_element_type=jnp.float32,
        ),
        "dp",
        scatter_dimension=0,
        tiled=True,
    )
    grad_b_rows = lax.all_gather(part_rows, "mp", axis=1, tiled=True)
    hidden_gradient = lax.dot_general(
        feature_rows, down_weight, (((1,), (1,)), ((), ())), preferred_element_type=jnp.float32
    )
    hidden_gradient = hidden_gradient + lax.dot_general(
        passed_through, adapter_first, (((1,), (1,)), ((), ())), preferred_element_type=jnp.float32
    )
    grad_gate = (
        hidden_gradient * up_vals * sigmoid_gate * (1.0 + gate_vals * (1.0 - sigmoid_gate))
    ).astype(jnp.bfloat16)
    grad_up = (hidden_gradient * silu_gate).astype(jnp.bfloat16)
    return (grad_gate, grad_up, grad_a_rows[None], grad_b_rows)


def solution(mesh):
    return jax.shard_map(
        body,
        mesh=mesh,
        in_specs=(
            P("dp", "mp"),
            P("dp", "mp"),
            P("dp", "mp"),
            P("mp", None),
            P("mp", None),
            P(),
            P("dp"),
        ),
        out_specs=(P("dp", "mp"), P("dp", "mp"), P("mp", "dp", None), P("dp", None)),
        check_vma=False,
    )
```

profile of v0, /device:TPU:0, one launch (start us, length us, event | category | flops | bytes accessed | tf_op | source)
XLA Modules:
  0.0 165.8 jit_solution(9476661914861650010)
XLA Ops:
  7.2 0.0 copy-start
  7.2 0.9 convert_reduce_fusion.1
  8.1 0.7 multiply_add_fusion
  8.8 0.1 convert_reduce_fusion
  8.9 0.7 convert_element_type.87
  9.6 7.3 %all-to-all-start = ((bf16[8,3,1]{1,2,0:T(2,128)(2,1)}), bf16[8,3,1]{1,2,0:T(2,128)(2,1)S(1)}, u32[]{:S(2)}, u32[]{:S(2)}) async-start(bf16[8,3,1]{1,2,0:T(2,128)(2,1)} %convert_element_type.87), calls=%async_computation | async-start | bytes 8192 | tf_op jit(solution)/shard_map/all_to_all | solution.py:35
  16.9 1.1 reshape.77
  18.0 0.2 convolution_convert_fusion.1
  18.3 1.0 all_to_all.13
  19.2 4.1 %all-to-all-done = bf16[8,3,1]{1,2,0:T(2,128)(2,1)S(1)} async-done(((bf16[8,3,1]{1,2,0:T(2,128)(2,1)}), bf16[8,3,1]{1,2,0:T(2,128)(2,1)S(1)}, u32[]{:S(2)}, u32[]{:S(2)}) %all-to-all-start) | async-done | bytes 80 | tf_op jit(solution)/shard_map/all_to_all | solution.py:35
  23.3 3.5 %all-to-all-start.1 = ((bf16[8,3,7168]{2,1,0:T(4,128)(2,1)}), bf16[8,3,7168]{2,1,0:T(4,128)(2,1)S(1)}, u32[]{:S(2)}, u32[]{:S(2)}) async-start(bf16[8,3,7168]{2,1,0:T(4,128)(2,1)} %all_to_all.13), calls=%async_computation.1 | async-start | bytes 917504 | tf_op jit(solution)/shard_map/all_to_all | solution.py:34
  26.8 0.0 all-gather.2.cloned.1.call-start
  26.9 0.1 reshape.80
  27.0 0.1 gt.12
  27.1 0.1 add_reduce_fusion
  27.2 11.4 %all-to-all-done.1 = bf16[8,3,7168]{2,1,0:T(4,128)(2,1)S(1)} async-done(((bf16[8,3,7168]{2,1,0:T(4,128)(2,1)}), bf16[8,3,7168]{2,1,0:T(4,128)(2,1)S(1)}, u32[]{:S(2)}, u32[]{:S(2)}) %all-to-all-start.1) | async-done | bytes 344096 | tf_op jit(solution)/shard_map/all_to_all | solution.py:34
  38.6 0.3 all_to_all.15
  38.9 0.2 convolution_convert_fusion
  39.2 0.9 reshape.78
  40.1 0.0 all-gather.2.cloned.1.call-update
  40.1 0.0 all-reduce.5.cloned.1.call-start
  40.1 17.7 %all-gather.2.cloned.1.call-done = bf16[192,3584]{1,0:T(8,128)(2,1)} async-done(((bf16[192,896]{1,0:T(8,128)(2,1)}), bf16[192,3584]{1,0:T(8,128)(2,1)}) %all-gather.2.cloned.1.call-update) | async-done | bytes 1376272 | tf_op jit(solution)/shard_map/all_gather | solution.py:45
  57.9 0.0 copy-done
  57.9 0.0 copy-start.2
  57.9 1.9 %convolution_convert_fusion.2 = bf16[192,96]{1,0:T(8,128)(2,1)S(1)} fusion(bf16[192,3584]{1,0:T(8,128)(2,1)} %all-gather.2.cloned.1.call-done, bf16[96,3584]{1,0:T(8,128)(2,1)S(1)} %copy-done), kind=kOutput, calls=%fused_computation.17 | convolution fusion | flops 132139008 | bytes 2101248 | tf_op jit(solution)/shard_map/dot_general | solution.py:53
  59.8 0.0 copy-done.2
  59.8 0.0 copy-start.3
  59.8 10.8 %fusion.18 = f32[192,2496]{1,0:T(8,128)} fusion(bf16[192,3584]{1,0:T(8,128)(2,1)S(1)} %copy-done.2, bf16[2496,3584]{1,0:T(8,128)(2,1)} %param.10), kind=kOutput, calls=%fused_computation.37 | convolution fusion | flops 3435134976 | bytes 21184512 | tf_op jit(solution)/shard_map/dot_general | solution.py:79
  70.7 0.0 copy-done.3
  70.7 4.7 %multiply_convert_fusion = (bf16[192,2496]{1,0:T(8,128)(2,1)}, bf16[192,2496]{1,0:T(8,128)(2,1)}, bf16[192,2496]{1,0:T(8,128)(2,1)S(1)}) fusion(bf16[192,2496]{1,0:T(8,128)(2,1)} %param.8, bf16[192,2496]{1,0:T(8,128)(2,1)} %param.9, f32[192,2496]{1,0:T(8,128)} %fusion.18, bf16[192,96]{1,0:T(8,128)(2,1)S(1)} %convolution_convert_fusion.2, ...), kind=kOutput, calls=%fused_computation.16 | convolution fusion | flops 100638720 | bytes 7225344 | tf_op jit(solution)/shard_map/dot_general | solution.py:82
  75.4 1.3 fusion.19
  76.7 0.0 all-reduce.5.cloned.1.call-update
  76.7 0.4 fusion.20
  77.2 11.6 %psum.7 = bf16[192,96]{1,0:T(8,128)(2,1)S(1)} all-reduce(f32[192,96]{1,0:T(8,128)S(1)} %fusion.20), channel_id=1, replica_groups=mesh['dp'=8,'mp'=4] {'mp'}, use_global_device_ids=true, to_apply=%region_4.5 | all-reduce | flops 18432 | bytes 110592 | tf_op jit(solution)/shard_map/psum | solution.py:52
  88.8 0.0 copy-done.1
  88.8 0.2 fusion.21
  89.0 25.9 %fusion = f32[16,896]{1,0:T(8,128)S(1)} fusion(f32[96,896]{1,0:T(8,128)S(1)} %fusion.21), kind=kCustom, calls=%all-reduce-scatter | all-reduce-scatter fusion | flops 114689 | bytes 401920
  114.9 2.4 %collective-permute-start = (f32[16,896]{1,0:T(8,128)S(1)}, f32[16,896]{1,0:T(8,128)S(1)}, u32[]{:S(2)}, u32[]{:S(2)}) collective-permute-start(f32[16,896]{1,0:T(8,128)S(1)} %fusion), channel_id=1, source_target_pairs={{0,4},{4,8},{8,12},{12,16},{16,20},{20,24},{24,28},{1,5},{5,9},{9,... | collective-permute-start | bytes 172040
  117.3 3.2 %collective-permute-start.1 = (f32[12,896]{1,0:T(8,128)S(1)}, f32[12,896]{1,0:T(8,128)S(1)}, u32[]{:S(2)}, u32[]{:S(2)}) collective-permute-start(f32[12,896]{1,0:T(8,128)S(1)} %slice), channel_id=1, source_target_pairs={{0,8},{4,12},{8,16},{12,20},{16,24},{20,28},{1,9},{5,13},{9,17},{1... | collective-permute-start | bytes 129032
  120.5 0.0 copy-done.4
  120.5 0.6 fusion.17
  122.4 0.0 collective-permute-done.1
  122.4 0.0 collective-permute-done
  122.4 0.3 concatenate
  122.7 5.7 %all_gather.7 = f32[12,3584]{1,0:T(8,128)S(1)} all-gather(f32[12,896]{1,0:T(8,128)S(1)} %constant_dynamic-slice_fusion), channel_id=1, replica_groups=mesh['dp'=8,'mp'=4] {'mp'}, dimensions={1}, use_global_device_ids=true | all-gather | bytes 215040 | tf_op jit(solution)/shard_map/all_gather | solution.py:78
  128.4 28.2 %all-reduce.5.cloned.1.call-done = f32[2496,96]{0,1:T(8,128)} async-done(((f32[2496,96]{0,1:T(8,128)}), f32[2496,96]{0,1:T(8,128)}) %all-reduce.5.cloned.1.call-update) | async-done | bytes 958480
  156.6 1.7 %dynamic-slice_bitcast_fusion = f32[1,312,96]{1,2,0:T(8,128)} fusion(f32[2496,96]{0,1:T(8,128)} %all-reduce.5.cloned.1.call-done, u32[]{:T(128)S(6)} %multiply.1), kind=kLoop, calls=%fused_computation.18 | loop fusion | bytes 239620 | tf_op jit(solution)/shard_map/broadcast_in_dim | solution.py:89
  158.3 0.7 copy.21
  (7 shorter events, 0.1 us)
Async XLA Ops:
  7.2 50.7 %copy-start = (bf16[96,3584]{1,0:T(8,128)(2,1)S(1)}, bf16[96,3584]{1,0:T(8,128)(2,1)}, u32[]{:S(2)}) copy-start(bf16[96,3584]{1,0:T(8,128)(2,1)} %param.12) | copy-start | bytes 2064388
  9.6 13.7 %all-to-all-start = ((bf16[8,3,1]{1,2,0:T(2,128)(2,1)}), bf16[8,3,1]{1,2,0:T(2,128)(2,1)S(1)}, u32[]{:S(2)}, u32[]{:S(2)}) async-start(bf16[8,3,1]{1,2,0:T(2,128)(2,1)} %convert_element_type.87), calls=%async_computation | async-start | bytes 8192 | tf_op jit(solution)/shard_map/all_to_all | solution.py:35
  23.3 15.3 %all-to-all-start.1 = ((bf16[8,3,7168]{2,1,0:T(4,128)(2,1)}), bf16[8,3,7168]{2,1,0:T(4,128)(2,1)S(1)}, u32[]{:S(2)}, u32[]{:S(2)}) async-start(bf16[8,3,7168]{2,1,0:T(4,128)(2,1)} %all_to_all.13), calls=%async_computation.1 | async-start | bytes 917504 | tf_op jit(solution)/shard_map/all_to_all | solution.py:34
  26.8 31.1 %all-gather.2.cloned.1.call-start = ((), (), s32[]{:S(2)}) async-start(), calls=%async_computation.2 | async-start | bytes 1720320 | tf_op jit(solution)/shard_map/all_gather | solution.py:45
  40.1 116.5 %all-reduce.5.cloned.1.call-start = ((), (), s32[]{:S(2)}) async-start(), calls=%async_computation.3 | async-start | bytes 1966080
  57.9 2.0 %copy-start.2 = (bf16[192,3584]{1,0:T(8,128)(2,1)S(1)}, bf16[192,3584]{1,0:T(8,128)(2,1)}, u32[]{:S(2)}) copy-start(bf16[192,3584]{1,0:T(8,128)(2,1)} %all-gather.2.cloned.1.call-done) | copy-start | bytes 4128772
  59.8 10.8 %copy-start.3 = (bf16[2496,96]{0,1:T(8,128)(2,1)S(1)}, bf16[2496,96]{0,1:T(8,128)(2,1)}, u32[]{:S(2)}) copy-start(bf16[2496,96]{0,1:T(8,128)(2,1)} %param.11) | copy-start | bytes 1437700
  75.4 13.4 %copy-start.1 = (bf16[192,896]{1,0:T(8,128)(2,1)S(1)}, bf16[192,896]{1,0:T(8,128)(2,1)}, u32[]{:S(2)}) copy-start(bf16[192,896]{1,0:T(8,128)(2,1)} %reshape.78) | copy-start | bytes 1032196
  76.7 43.8 %copy-start.4 = (u32[32]{0:T(128)S(1)}, u32[32]{0:T(128)}, u32[]{:S(2)}) copy-start(u32[32]{0:T(128)} %constant.17) | copy-start | bytes 388
  114.9 7.5 %collective-permute-start = (f32[16,896]{1,0:T(8,128)S(1)}, f32[16,896]{1,0:T(8,128)S(1)}, u32[]{:S(2)}, u32[]{:S(2)}) collective-permute-start(f32[16,896]{1,0:T(8,128)S(1)} %fusion), channel_id=1, source_target_pairs={{0,4},{4,8},{8,12},{12,16},{16,20},{20,24},{24,28},{1,5},{5,9},{9,... | collective-permute-start | bytes 172040
  117.3 5.1 %collective-permute-start.1 = (f32[12,896]{1,0:T(8,128)S(1)}, f32[12,896]{1,0:T(8,128)S(1)}, u32[]{:S(2)}, u32[]{:S(2)}) collective-permute-start(f32[12,896]{1,0:T(8,128)S(1)} %slice), channel_id=1, source_target_pairs={{0,8},{4,12},{8,16},{12,20},{16,24},{20,28},{1,9},{5,13},{9,17},{1... | collective-permute-start | bytes 129032
Sparse Core Ops, SparseCore 0:
  40.2 17.5 all-gather.1
  76.9 79.7 all-reduce.4
where the time goes:
time: 166 us
  waiting for transfers between devices  61.4 us (37%)
  blocking collectives  43.2 us (26%)
  matrix products  19.9 us (12%)
  starting transfers between devices  16.4 us (10%)
  between operations  15.5 us (9%)
  local copies, waits for them, and re-layouts  7.48 us (5%)
  other arithmetic  1.9 us (1%)
    unnamed x5, waiting for transfers between devices  28.2 us
    unnamed x1, blocking collectives  25.9 us
    all_gather x1, waiting for transfers between devices, body(): feature_rows = lax.all_gather(packed_tokens, 'mp', axis=1, tiled=True)  17.7 us
    psum x1, blocking collectives, body(): low_rank_rows = lax.psum(low_rank_piece, 'mp').astype(jnp.bfloat16)  11.6 us
    all_to_all x1, waiting for transfers between devices, body(): lax.all_to_all(outgoing, 'dp', split_axis=0, concat_axis=0, tiled=True)  11.4 us
    dot_general x1, matrix products, body(): lax.dot_general(feature_rows, down_weight, (((1,), (1,)), ((), ())), pref...  10.8 us
    all_to_all x1, starting transfers between devices, body(): lax.all_to_all(filled, 'dp', split_axis=0, concat_axis=0, tiled=True)  7.31 us
    all_gather x1, blocking collectives, body(): grad_b_rows = lax.all_gather(part_rows, 'mp', axis=1, tiled=True)  5.69 us
  transfers between devices with their start and end apart: 6, of which 4 were waited for; matrix products, arithmetic and copies ran while one was open for 18% of the time, Pallas kernels for 0%

commit v1 on v0

--- a/solution.py
+++ b/solution.py
@@ -42,7 +42,12 @@
         .astype(jnp.bfloat16)
         .reshape(tokens_here, feature_cols)
     )
-    feature_rows = lax.all_gather(packed_tokens, "mp", axis=1, tiled=True)
+    ring = [packed_tokens]
+    for hop in range(3):
+        ring.append(lax.ppermute(ring[-1], "mp", [(dev, (dev + 1) % 4) for dev in range(4)]))
+    feature_rows = jnp.roll(
+        jnp.concatenate(ring[::-1], axis=1), (lax.axis_index("mp") + 1) * ring[0].shape[1], axis=1
+    )
     gate_vals = gate_preactivation.astype(jnp.float32)
     up_vals = up_preactivation.astype(jnp.float32)
     sigmoid_gate = jax.nn.sigmoid(gate_vals)

time: 166 us -> 162 us (0.976)
  matrix products: 19.9 us -> 14.9 us
  waiting for transfers between devices: 61.4 us -> 64.2 us
    ppermute x0 -> x3, waiting for transfers between devices: none -> 20 us  [body(): lax.ppermute(ring[-1], 'mp', [(dev, (dev + 1) % 4) for dev in range(4)])]
    all_gather x1 -> x0, waiting for transfers between devices: 17.7 us -> none  [body(): feature_rows = lax.all_gather(packed_tokens, 'mp', axis=1, tiled=True)]
    dot_general x1, matrix products: 4.7 us -> 0.4 us  [body(): lax.dot_general(passed_through, adapter_first, (((1,), (1,)), ((), ())),...]
    unnamed x5 -> x4, waiting for transfers between devices: 28.2 us -> 28.7 us
  transfers between devices with their start and end apart: 6 -> 8, of which waited for: 4 -> 6; matrix products, arithmetic and copies ran while one was open for 18% -> 17% of each run, Pallas kernels for 0% -> 0%
where the time goes in v1:
time: 162 us; the launch traced here: 161 us
  waiting for transfers between devices  64.2 us (40%)
  blocking collectives  42.2 us (26%)
  between operations  15.6 us (10%)
  starting transfers between devices  15.2 us (9%)
  matrix products  14.9 us (9%)
  local copies, waits for them, and re-layouts  7.45 us (5%)
  other arithmetic  1.9 us (1%)
    unnamed x4, waiting for transfers between devices  28.7 us
    unnamed x1, blocking collectives  24.6 us
    ppermute x3, waiting for transfers between devices, body(): lax.ppermute(ring[-1], 'mp', [(dev, (dev + 1) % 4) for dev in range(4)])  20 us
    psum x1, blocking collectives, body(): low_rank_rows = lax.psum(low_rank_piece, 'mp').astype(jnp.bfloat16)  11.5 us
    all_to_all x1, waiting for transfers between devices, body(): lax.all_to_all(outgoing, 'dp', split_axis=0, concat_axis=0, tiled=True)  11.4 us
    dot_general x1, matrix products, body(): lax.dot_general(feature_rows, down_weight, (((1,), (1,)), ((), ())), pref...  11.3 us
    all_to_all x1, starting transfers between devices, body(): lax.all_to_all(filled, 'dp', split_axis=0, concat_axis=0, tiled=True)  7.31 us
    all_gather x1, blocking collectives, body(): grad_b_rows = lax.all_gather(part_rows, 'mp', axis=1, tiled=True)  6.14 us
  transfers between devices with their start and end apart: 8, of which 6 were waited for; matrix products, arithmetic and copies ran while one was open for 17% of the time, Pallas kernels for 0%

profile of v1, /device:TPU:0, one launch (start us, length us, event | category | flops | bytes accessed | tf_op | source)
XLA Modules:
  0.0 161.5 jit_solution(3934705202072427684)
XLA Ops:
  7.2 0.0 copy-start
  7.2 0.9 convert_reduce_fusion.1
  8.1 0.7 multiply_add_fusion
  8.8 0.1 convert_reduce_fusion
  8.9 0.7 convert_element_type.87
  9.6 7.3 %all-to-all-start = ((bf16[8,3,1]{1,2,0:T(2,128)(2,1)}), bf16[8,3,1]{1,2,0:T(2,128)(2,1)S(1)}, u32[]{:S(2)}, u32[]{:S(2)}) async-start(bf16[8,3,1]{1,2,0:T(2,128)(2,1)} %convert_element_type.87), calls=%async_computation | async-start | bytes 8192 | tf_op jit(solution)/shard_map/all_to_all | solution.py:35
  16.9 1.1 reshape.77
  18.0 0.2 convolution_convert_fusion.1
  18.3 1.0 all_to_all.13
  19.2 4.1 %all-to-all-done = bf16[8,3,1]{1,2,0:T(2,128)(2,1)S(1)} async-done(((bf16[8,3,1]{1,2,0:T(2,128)(2,1)}), bf16[8,3,1]{1,2,0:T(2,128)(2,1)S(1)}, u32[]{:S(2)}, u32[]{:S(2)}) %all-to-all-start) | async-done | bytes 80 | tf_op jit(solution)/shard_map/all_to_all | solution.py:35
  23.3 3.5 %all-to-all-start.1 = ((bf16[8,3,7168]{2,1,0:T(4,128)(2,1)}), bf16[8,3,7168]{2,1,0:T(4,128)(2,1)S(1)}, u32[]{:S(2)}, u32[]{:S(2)}) async-start(bf16[8,3,7168]{2,1,0:T(4,128)(2,1)} %all_to_all.13), calls=%async_computation.1 | async-start | bytes 917504 | tf_op jit(solution)/shard_map/all_to_all | solution.py:34
  26.8 0.0 all-reduce.5.cloned.1.call-start
  26.9 0.1 reshape.80
  27.0 0.1 gt.12
  27.1 0.1 add_reduce_fusion
  27.2 11.4 %all-to-all-done.1 = bf16[8,3,7168]{2,1,0:T(4,128)(2,1)S(1)} async-done(((bf16[8,3,7168]{2,1,0:T(4,128)(2,1)}), bf16[8,3,7168]{2,1,0:T(4,128)(2,1)S(1)}, u32[]{:S(2)}, u32[]{:S(2)}) %all-to-all-start.1) | async-done | bytes 344096 | tf_op jit(solution)/shard_map/all_to_all | solution.py:34
  38.6 0.3 all_to_all.15
  38.9 0.2 convolution_convert_fusion
  39.2 0.2 reshape.78
  39.3 0.1 collective-permute-start
  39.4 6.7 %collective-permute-done = bf16[192,896]{1,0:T(8,128)(2,1)S(1)} collective-permute-done((bf16[192,896]{1,0:T(8,128)(2,1)S(1)}, bf16[192,896]{1,0:T(8,128)(2,1)S(1)}, u32[]{:S(2)}, u32[]{:S(2)}) %collective-permute-start) | collective-permute-done | bytes 344096 | tf_op jit(solution)/shard_map/ppermute | solution.py:47
  46.1 6.7 %collective-permute-done.1 = bf16[192,896]{1,0:T(8,128)(2,1)S(1)} collective-permute-done((bf16[192,896]{1,0:T(8,128)(2,1)S(1)}, bf16[192,896]{1,0:T(8,128)(2,1)S(1)}, u32[]{:S(2)}, u32[]{:S(2)}) %collective-permute-start.1) | collective-permute-done | bytes 344096 | tf_op jit(solution)/shard_map/ppermute | solution.py:47
  52.7 6.7 %collective-permute-done.2 = bf16[192,896]{1,0:T(8,128)(2,1)S(1)} collective-permute-done((bf16[192,896]{1,0:T(8,128)(2,1)S(1)}, bf16[192,896]{1,0:T(8,128)(2,1)S(1)}, u32[]{:S(2)}, u32[]{:S(2)}) %collective-permute-start.2) | collective-permute-done | bytes 344096 | tf_op jit(solution)/shard_map/ppermute | solution.py:47
  59.5 0.1 constant_dynamic-update-slice_fusion.5
  59.6 0.1 constant_dynamic-update-slice_fusion.4
  59.6 0.1 constant_dynamic-update-slice_fusion.3
  59.7 0.1 constant_dynamic-update-slice_fusion.2
  59.8 0.1 constant_dynamic-update-slice_fusion.1
  59.8 0.1 constant_dynamic-update-slice_fusion
  59.9 0.7 fusion.12
  60.6 0.4 fusion.26
  61.0 0.0 copy-done.3
  61.1 0.3 copy-done.4
  61.4 11.3 %multiply_convert_fusion = (bf16[192,2496]{1,0:T(8,128)(2,1)}, bf16[192,2496]{1,0:T(8,128)(2,1)}, bf16[192,2496]{1,0:T(8,128)(2,1)S(1)}) fusion(bf16[192,2496]{1,0:T(8,128)(2,1)S(1)} %copy-done.3, bf16[192,2496]{1,0:T(8,128)(2,1)S(1)} %copy-done.4, f32[192,2496]{1,0:T(8,128)S(1)} %fusion.26, bf16[2496,3584]{1,0:T(8,128)(2,1)} %param.10, ...), kind=kOutput, calls=%fused_computation.16 | convolution fusion | flops 3443761152 | bytes 26075140 | tf_op jit(solution)/shard_map/dot_general | solution.py:84
  72.7 1.3 fusion.27
  74.0 0.0 all-reduce.5.cloned.1.call-update
  74.1 0.4 fusion.28
  74.5 11.5 %psum.7 = bf16[192,96]{1,0:T(8,128)(2,1)S(1)} all-reduce(f32[192,96]{1,0:T(8,128)S(1)} %fusion.28), channel_id=1, replica_groups=mesh['dp'=8,'mp'=4] {'mp'}, use_global_device_ids=true, to_apply=%region_4.5 | all-reduce | flops 18432 | bytes 110592 | tf_op jit(solution)/shard_map/psum | solution.py:57
  86.0 0.2 fusion.29
  86.3 24.6 %fusion = f32[16,896]{1,0:T(8,128)S(1)} fusion(f32[96,896]{1,0:T(8,128)S(1)} %fusion.29), kind=kCustom, calls=%all-reduce-scatter | all-reduce-scatter fusion | flops 114689 | bytes 401920
  110.8 3.1 %collective-permute-start.3 = (f32[16,896]{1,0:T(8,128)S(1)}, f32[16,896]{1,0:T(8,128)S(1)}, u32[]{:S(2)}, u32[]{:S(2)}) collective-permute-start(f32[16,896]{1,0:T(8,128)S(1)} %fusion), channel_id=1, source_target_pairs={{0,4},{4,8},{8,12},{12,16},{16,20},{20,24},{24,28},{1,5},{5,9},{9,... | collective-permute-start | bytes 172040
  113.9 1.3 collective-permute-start.4
  115.2 0.6 fusion.25
  117.1 0.3 concatenate.7
  117.5 6.1 %all_gather.3 = f32[12,3584]{1,0:T(8,128)S(1)} all-gather(f32[12,896]{1,0:T(8,128)S(1)} %constant_dynamic-slice_fusion), channel_id=1, replica_groups=mesh['dp'=8,'mp'=4] {'mp'}, dimensions={1}, use_global_device_ids=true | all-gather | bytes 215040 | tf_op jit(solution)/shard_map/all_gather | solution.py:83
  123.6 28.7 %all-reduce.5.cloned.1.call-done = f32[2496,96]{0,1:T(8,128)} async-done(((f32[2496,96]{0,1:T(8,128)}), f32[2496,96]{0,1:T(8,128)}) %all-reduce.5.cloned.1.call-update) | async-done | bytes 958480
  152.3 1.7 %dynamic-slice_bitcast_fusion = f32[1,312,96]{1,2,0:T(8,128)} fusion(f32[2496,96]{0,1:T(8,128)} %all-reduce.5.cloned.1.call-done, u32[]{:T(128)S(6)} %multiply.1), kind=kLoop, calls=%fused_computation.21 | loop fusion | bytes 239620 | tf_op jit(solution)/shard_map/broadcast_in_dim | solution.py:94
  154.0 0.7 copy.28
  (18 shorter events, 0.2 us)
Async XLA Ops:
  7.2 52.7 %copy-start = (bf16[96,3584]{1,0:T(8,128)(2,1)S(1)}, bf16[96,3584]{1,0:T(8,128)(2,1)}, u32[]{:S(2)}) copy-start(bf16[96,3584]{1,0:T(8,128)(2,1)} %param.12) | copy-start | bytes 2064388
  9.6 13.7 %all-to-all-start = ((bf16[8,3,1]{1,2,0:T(2,128)(2,1)}), bf16[8,3,1]{1,2,0:T(2,128)(2,1)S(1)}, u32[]{:S(2)}, u32[]{:S(2)}) async-start(bf16[8,3,1]{1,2,0:T(2,128)(2,1)} %convert_element_type.87), calls=%async_computation | async-start | bytes 8192 | tf_op jit(solution)/shard_map/all_to_all | solution.py:35
  23.3 15.3 %all-to-all-start.1 = ((bf16[8,3,7168]{2,1,0:T(4,128)(2,1)}), bf16[8,3,7168]{2,1,0:T(4,128)(2,1)S(1)}, u32[]{:S(2)}, u32[]{:S(2)}) async-start(bf16[8,3,7168]{2,1,0:T(4,128)(2,1)} %all_to_all.13), calls=%async_computation.1 | async-start | bytes 917504 | tf_op jit(solution)/shard_map/all_to_all | solution.py:34
  26.8 125.5 %all-reduce.5.cloned.1.call-start = ((), (), s32[]{:S(2)}) async-start(), calls=%async_computation.2 | async-start | bytes 1966080
  39.3 6.7 %collective-permute-start = (bf16[192,896]{1,0:T(8,128)(2,1)S(1)}, bf16[192,896]{1,0:T(8,128)(2,1)S(1)}, u32[]{:S(2)}, u32[]{:S(2)}) collective-permute-start(bf16[192,896]{1,0:T(8,128)(2,1)S(1)} %reshape.78), channel_id=1, source_target_pairs={{0,1},{1,2},{2,3},{3,0},{4,5},{5,6},{6,7},{7,4},{8,9},{9,10},{10,1... | collective-permute-start | bytes 1032200 | tf_op jit(solution)/shard_map/ppermute | solution.py:47
  46.1 6.7 %collective-permute-start.1 = (bf16[192,896]{1,0:T(8,128)(2,1)S(1)}, bf16[192,896]{1,0:T(8,128)(2,1)S(1)}, u32[]{:S(2)}, u32[]{:S(2)}) collective-permute-start(bf16[192,896]{1,0:T(8,128)(2,1)S(1)} %collective-permute-done), channel_id=1, source_target_pairs={{0,1},{1,2},{2,3},{3,0},{4,5},{5,6},{6,7},{7,4},{8,9},{9,10},{10,1... | collective-permute-start | bytes 1032200 | tf_op jit(solution)/shard_map/ppermute | solution.py:47
  52.7 6.7 %collective-permute-start.2 = (bf16[192,896]{1,0:T(8,128)(2,1)S(1)}, bf16[192,896]{1,0:T(8,128)(2,1)S(1)}, u32[]{:S(2)}, u32[]{:S(2)}) collective-permute-start(bf16[192,896]{1,0:T(8,128)(2,1)S(1)} %collective-permute-done.1), channel_id=1, source_target_pairs={{0,1},{1,2},{2,3},{3,0},{4,5},{5,6},{6,7},{7,4},{8,9},{9,10},{10,1... | collective-permute-start | bytes 1032200 | tf_op jit(solution)/shard_map/ppermute | solution.py:47
  59.6 1.1 copy-start.1
  59.8 1.2 copy-start.3
  59.8 1.5 copy-start.4
  72.7 42.5 %copy-start.2 = (u32[32]{0:T(128)S(1)}, u32[32]{0:T(128)}, u32[]{:S(2)}) copy-start(u32[32]{0:T(128)} %constant.43) | copy-start | bytes 388
  110.8 6.3 %collective-permute-start.3 = (f32[16,896]{1,0:T(8,128)S(1)}, f32[16,896]{1,0:T(8,128)S(1)}, u32[]{:S(2)}, u32[]{:S(2)}) collective-permute-start(f32[16,896]{1,0:T(8,128)S(1)} %fusion), channel_id=1, source_target_pairs={{0,4},{4,8},{8,12},{12,16},{16,20},{20,24},{24,28},{1,5},{5,9},{9,... | collective-permute-start | bytes 172040
  113.9 3.2 %collective-permute-start.4 = (f32[12,896]{1,0:T(8,128)S(1)}, f32[12,896]{1,0:T(8,128)S(1)}, u32[]{:S(2)}, u32[]{:S(2)}) collective-permute-start(f32[12,896]{1,0:T(8,128)S(1)} %slice), channel_id=1, source_target_pairs={{0,8},{4,12},{8,16},{12,20},{16,24},{20,28},{1,9},{5,13},{9,17},{1... | collective-permute-start | bytes 129032
Sparse Core Ops, SparseCore 0:
  74.2 78.0 all-reduce.4
